TPU v7x, 512 devices: a whole 4x8x8 slice. The times are simulated.
512 devices in a mesh: tm: 32 (over z, x), frac: 16 (over y, core).
Axes of the slice: x: 4, y: 8, z: 8, core: 2. Of those that a mesh axis runs over, the one named last changes fastest.
Arguments:
- pressure0: float32 [64, 32, 128], P('frac'), may hold values from -6 to 6
- storage: float32 [64, 32, 128], P('frac'), may hold values from 0.1 to 1
- perm_base: float32 [64, 32, 128], P('frac'), may hold values from 0.2 to 5
- leakoff: float32 [64, 32, 128], P('frac'), may hold values from 0.5 to 2
- sources: float32 [32, 64, 32, 128], P('tm', 'frac'), may hold values from -6 to 6
- export_cells: int32 [4096], P('frac'), may hold values from 0 to 16383
- inter_local: int32 [16384], P('frac'), may hold values from 0 to 16383
- trace_source: int32 [16384], P('frac'), may hold values from 0 to 4095, as said below
- inter_trans: float32 [16384], P('frac'), may hold values from 0.5 to 4
- inter_count: int32 [16], P('frac'), may hold values from 1 to 1024, 8192 in all
Outputs:
- slice_pressure: float32 [32, 64, 32, 128], P('tm', 'frac')
Inputs may be any that keep to these rules, and one draw needn't show every extreme that they name: An entry of frac index d names a slot of another frac index: trace_source // 256 differs from d. `inter_count`: the live entries of a frac index are its first ones; the largest count is 1024.
All inputs are finite; a program needn't handle non-finite values. No bound on the sum of `inter_count` on one device may be relied on, other than what follows from the above.
Results may differ from a plain program's by a relative error of at most 0.00002.
Values sent between devices are 32-bit elements; how exact they have to be, the bound alone decides.
A program may use at most 64 MiB of HBM per device.

v0:
```python
import jax
import jax.numpy as jnp
from jax import lax
from jax.sharding import PartitionSpec as P

FINE_STEPS = 4
SWEEPS = 8
COARSE_SWEEPS = 2
ITERS = 2
stress_factor = 0.15
fine_size = 0.25


def next_rows(array):
    return jnp.concatenate([array[:, 1:, :], jnp.zeros_like(array[:, :1, :])], axis=1)


def prev_rows(array):
    return jnp.concatenate([jnp.zeros_like(array[:, :1, :]), array[:, :-1, :]], axis=1)


def next_cols(array):
    return jnp.concatenate([array[:, :, 1:], jnp.zeros_like(array[:, :, :1])], axis=2)


def prev_cols(array):
    return jnp.concatenate([jnp.zeros_like(array[:, :, :1]), array[:, :, :-1]], axis=2)


def implicit(pressure, slice_source, step_size, sweeps, fields, couple):
    storage, perm_base, leakoff, tisum = fields
    permeability = perm_base * jnp.exp(stress_factor * pressure)
    row_index = lax.broadcasted_iota(jnp.int32, pressure.shape, 1)
    col_index = lax.broadcasted_iota(jnp.int32, pressure.shape, 2)
    face_rows = jnp.where(
        row_index < pressure.shape[1] - 1, 0.5 * (permeability + next_rows(permeability)), 0.0
    )
    face_cols = jnp.where(
        col_index < pressure.shape[2] - 1, 0.5 * (permeability + next_cols(permeability)), 0.0
    )
    storage_rate = storage / step_size
    diagonal_total = (
        storage_rate + leakoff + face_rows + prev_rows(face_rows) + face_cols + prev_cols(face_cols)
    )
    right_side = storage_rate * pressure + slice_source
    if couple is not None:
        diagonal_total = diagonal_total + tisum
        right_side = right_side + couple(pressure)

    def sweep(sweep_index, current):
        beside = face_rows * next_rows(current) + prev_rows(face_rows * current)
        beside = beside + face_cols * next_cols(current) + prev_cols(face_cols * current)
        return (right_side + beside) / diagonal_total

    return lax.fori_loop(0, sweeps, sweep, pressure)


def body(
    pressure0,
    storage,
    perm_base,
    leakoff,
    sources,
    export_cells,
    inter_local,
    trace_source,
    inter_trans,
    inter_count,
):
    slice_count = lax.axis_size("tm")
    slice_index = lax.axis_index("tm")
    own_source = sources[0]
    entry_index = lax.broadcasted_iota(jnp.int32, inter_local.shape, 0)
    weights = jnp.where(entry_index < inter_count[0], inter_trans, jnp.zeros_like(inter_trans))
    cell_total = pressure0.size
    tisum = (
        jnp.zeros((cell_total,), jnp.float32).at[inter_local].add(weights).reshape(pressure0.shape)
    )
    fields = (storage, perm_base, leakoff, tisum)

    def couple(current):
        flat_field = current.reshape(-1)
        exported = flat_field[export_cells]
        gathered = lax.all_gather(exported, "frac", axis=0, tiled=True)
        remote_values = gathered[trace_source]
        return (
            jnp.zeros_like(flat_field)
            .at[inter_local]
            .add(weights * remote_values)
            .reshape(current.shape)
        )

    def coarse(pressure, slice_source):
        return implicit(pressure, slice_source, fine_size * FINE_STEPS, COARSE_SWEEPS, fields, None)

    all_sources = lax.all_gather(sources, "tm", axis=0, tiled=True)

    def chain(correction, carry_zero):
        if carry_zero:
            all_corrections = jnp.zeros_like(all_sources)
        else:
            all_corrections = lax.all_gather(correction[None], "tm", axis=0, tiled=True)

        def turn(turn_index, carried):
            current, kept_state = carried
            slice_source = lax.dynamic_index_in_dim(all_sources, turn_index, 0, keepdims=False)
            added = lax.dynamic_index_in_dim(all_corrections, turn_index, 0, keepdims=False)
            current = coarse(current, slice_source) + added
            kept_state = jnp.where(slice_index == turn_index + 1, current, kept_state)
            return (current, kept_state)

        final_pair = lax.fori_loop(0, slice_count - 1, turn, (pressure0, pressure0))
        return final_pair[1]

    state = chain(jnp.zeros_like(pressure0), True)
    for iteration in range(ITERS):
        fine_pressure = state
        for step_number in range(FINE_STEPS):
            fine_pressure = implicit(fine_pressure, own_source, fine_size, SWEEPS, fields, couple)
        coarse_end = coarse(state, own_source)
        state = chain(fine_pressure - coarse_end, False)
    return state[None]


def solution(mesh):
    placed = (
        P("frac", None, None),
        P("frac", None, None),
        P("frac", None, None),
        P("frac", None, None),
        P("tm", "frac", None, None),
        P("frac"),
        P("frac"),
        P("frac"),
        P("frac"),
        P("frac"),
    )
    return jax.shard_map(
        body, mesh=mesh, in_specs=placed, out_specs=P("tm", "frac", None, None), check_vma=False
    )
```

profile of v0, /device:TPU:8, one launch (start us, length us, event | category | flops | bytes accessed | tf_op | source)
XLA Modules:
  0.0 733.0 jit_solution(9327614761849319025)
XLA Ops:
  11.1 88.0 %all-gather.22.cloned.1.call-done = f32[32,4,32,128]{3,2,1,0:T(8,128)} async-done(((f32[1,4,32,128]{3,2,1,0:T(8,128)}), f32[32,4,32,128]{3,2,1,0:T(8,128)}) %all-gather.22.cloned.1.call-update) | async-done | bytes 2097168 | tf_op jit(solution)/shard_map/all_gather | solution.py:96
  99.1 52.9 %while.235 = (s32[]{:T(128)}, f32[4,32,128]{2,1,0:T(8,128)S(1)}, f32[4,32,128]{2,1,0:T(8,128)S(1)}, f32[4,32,128]{2,1,0:T(8,128)}, f32[4,32,128]{2,1,0:T(8,128)}...) while((s32[]{:T(128)}, f32[4,32,128]{2,1,0:T(8,128)S(1)}, ...), condition=%wide.region_3.4_spmd, body=%wide.region_0.3_spmd.sunk | while | flops 392741 | bytes 2790472 | solution.py:112
  102.6 0.9 bitcast_add_fusion.20
  153.0 1.7 gather_fusion
  154.8 15.7 %all-gather.10 = f32[16,1,256]{2,1,0:T(1,128)S(1)} all-gather(f32[1,1,256]{2,1,0:T(1,128)S(1)} %bitcast.174), channel_id=2, replica_groups=mesh['tm'=32,'frac'=16] {'frac'}, dimensions={0}, use_global_device_ids=true | all-gather | bytes 17408 | tf_op jit(solution)/shard_map/all_gather | solution.py:84
  170.5 6.1 gather_fusion.1
  176.7 5.9 scatter_custom_fusion.1
  182.6 5.9 scatter_custom_fusion
  188.8 1.7 while.236
  190.5 1.7 gather_fusion.2
  192.2 16.0 %all-gather.11 = f32[16,1,256]{2,1,0:T(1,128)S(1)} all-gather(f32[1,1,256]{2,1,0:T(1,128)S(1)} %bitcast.175), channel_id=3, replica_groups=mesh['tm'=32,'frac'=16] {'frac'}, dimensions={0}, use_global_device_ids=true | all-gather | bytes 17408 | tf_op jit(solution)/shard_map/all_gather | solution.py:84
  208.2 6.1 gather_fusion.3
  214.4 5.9 scatter_custom_fusion.2
  220.6 1.7 while.237
  222.4 1.7 gather_fusion.4
  224.1 15.2 %all-gather.12 = f32[16,1,256]{2,1,0:T(1,128)S(1)} all-gather(f32[1,1,256]{2,1,0:T(1,128)S(1)} %bitcast.176), channel_id=4, replica_groups=mesh['tm'=32,'frac'=16] {'frac'}, dimensions={0}, use_global_device_ids=true | all-gather | bytes 17408 | tf_op jit(solution)/shard_map/all_gather | solution.py:84
  239.3 6.1 gather_fusion.5
  245.5 5.9 scatter_custom_fusion.3
  251.8 1.7 while.238
  253.5 1.7 gather_fusion.6
  255.2 15.1 %all-gather.13 = f32[16,1,256]{2,1,0:T(1,128)S(1)} all-gather(f32[1,1,256]{2,1,0:T(1,128)S(1)} %bitcast.177), channel_id=5, replica_groups=mesh['tm'=32,'frac'=16] {'frac'}, dimensions={0}, use_global_device_ids=true | all-gather | bytes 17408 | tf_op jit(solution)/shard_map/all_gather | solution.py:84
  270.3 6.1 gather_fusion.7
  276.5 5.9 scatter_custom_fusion.4
  283.1 1.7 while.239
  285.8 79.1 %all-gather.24.cloned.1.call-done = f32[128,32,128]{2,1,0:T(8,128)} async-done(((f32[4,32,128]{2,1,0:T(8,128)}), f32[128,32,128]{2,1,0:T(8,128)}) %all-gather.24.cloned.1.call-update) | async-done | bytes 2097168 | tf_op jit(solution)/shard_map/all_gather | solution.py:102
  364.9 77.4 %while.242 = (s32[]{:T(128)}, f32[4,32,128]{2,1,0:T(8,128)S(1)}, f32[4,32,128]{2,1,0:T(8,128)S(1)}, f32[4,32,128]{2,1,0:T(8,128)S(1)}, f32[4,32,128]{2,1,0:T(8,1...) while((s32[]{:T(128)}, f32[4,32,128]{2,1,0:T(8,128)S(1)}, ...), condition=%wide.region_22.23_spmd, body=%wide.region_19.22_spmd.sunk | while | flops 409125 | bytes 2921564 | solution.py:112
  442.4 1.7 gather_fusion.8
  444.1 15.7 %all-gather.14 = f32[16,1,256]{2,1,0:T(1,128)S(1)} all-gather(f32[1,1,256]{2,1,0:T(1,128)S(1)} %bitcast.178), channel_id=7, replica_groups=mesh['tm'=32,'frac'=16] {'frac'}, dimensions={0}, use_global_device_ids=true | all-gather | bytes 17408 | tf_op jit(solution)/shard_map/all_gather | solution.py:84
  459.8 6.1 gather_fusion.9
  466.0 5.9 scatter_custom_fusion.5
  472.3 1.7 while.243
  474.0 1.7 gather_fusion.10
  475.7 16.0 %all-gather.15 = f32[16,1,256]{2,1,0:T(1,128)S(1)} all-gather(f32[1,1,256]{2,1,0:T(1,128)S(1)} %bitcast.179), channel_id=8, replica_groups=mesh['tm'=32,'frac'=16] {'frac'}, dimensions={0}, use_global_device_ids=true | all-gather | bytes 17408 | tf_op jit(solution)/shard_map/all_gather | solution.py:84
  491.7 6.1 gather_fusion.11
  497.8 5.9 scatter_custom_fusion.6
  504.1 1.7 while.244
  505.8 1.7 gather_fusion.12
  507.6 15.2 %all-gather.16 = f32[16,1,256]{2,1,0:T(1,128)S(1)} all-gather(f32[1,1,256]{2,1,0:T(1,128)S(1)} %bitcast.180), channel_id=9, replica_groups=mesh['tm'=32,'frac'=16] {'frac'}, dimensions={0}, use_global_device_ids=true | all-gather | bytes 17408 | tf_op jit(solution)/shard_map/all_gather | solution.py:84
  522.8 6.1 gather_fusion.13
  529.0 5.9 scatter_custom_fusion.7
  535.2 1.7 while.245
  536.9 1.7 gather_fusion.14
  538.7 15.1 %all-gather.17 = f32[16,1,256]{2,1,0:T(1,128)S(1)} all-gather(f32[1,1,256]{2,1,0:T(1,128)S(1)} %bitcast.173), channel_id=10, replica_groups=mesh['tm'=32,'frac'=16] {'frac'}, dimensions={0}, use_global_device_ids=true | all-gather | bytes 17408 | tf_op jit(solution)/shard_map/all_gather | solution.py:84
  553.8 6.1 gather_fusion.15
  559.9 5.9 scatter_custom_fusion.8
  566.6 1.7 while.246
  569.0 79.4 %all-gather.26.cloned.1.call-done = f32[128,32,128]{2,1,0:T(8,128)} async-done(((f32[4,32,128]{2,1,0:T(8,128)}), f32[128,32,128]{2,1,0:T(8,128)}) %all-gather.26.cloned.1.call-update) | async-done | bytes 2097168 | tf_op jit(solution)/shard_map/all_gather | solution.py:102
  648.4 77.4 %while.249 = (s32[]{:T(128)}, f32[4,32,128]{2,1,0:T(8,128)S(1)}, f32[4,32,128]{2,1,0:T(8,128)S(1)}, f32[4,32,128]{2,1,0:T(8,128)S(1)}, f32[4,32,128]{2,1,0:T(8,1...) while((s32[]{:T(128)}, f32[4,32,128]{2,1,0:T(8,128)S(1)}, ...), condition=%wide.region_40.41_spmd, body=%wide.region_37.40_spmd.sunk | while | flops 409125 | bytes 2921564 | solution.py:112
  (1683 shorter events, 260.9 us)
Async XLA Ops:
  6.5 92.6 %all-gather.22.cloned.1.call-start = ((), (), s32[]{:S(2)}) async-start(), calls=%async_computation | async-start | bytes 2162688 | tf_op jit(solution)/shard_map/all_gather | solution.py:96
  7.4 357.5 %all-gather.24.cloned.1.call-start = ((), (), s32[]{:S(2)}) async-start(), calls=%async_computation.1 | async-start | bytes 2162688 | tf_op jit(solution)/shard_map/all_gather | solution.py:102
  170.5 6.2 copy-start.5
  170.5 18.2 %copy-start = (f32[4,32,128]{2,1,0:T(8,128)S(1)}, f32[4,32,128]{2,1,0:T(8,128)}, u32[]{:S(2)}) copy-start(f32[4,32,128]{2,1,0:T(8,128)} %get-tuple-element.2573) | copy-start | bytes 196612
  170.5 18.2 %copy-start.2 = (f32[1,4,32,128]{3,2,1,0:T(8,128)S(1)}, f32[1,4,32,128]{3,2,1,0:T(8,128)}, u32[]{:S(2)}) copy-start(f32[1,4,32,128]{3,2,1,0:T(8,128)} %param.46) | copy-start | bytes 196612
  170.5 18.2 %copy-start.4 = (f32[4,32,128]{2,1,0:T(8,128)S(1)}, f32[4,32,128]{2,1,0:T(8,128)}, u32[]{:S(2)}) copy-start(f32[4,32,128]{2,1,0:T(8,128)} %param.45) | copy-start | bytes 196612
  208.2 12.1 %copy-start.1 = (f32[4,32,128]{2,1,0:T(8,128)S(1)}, f32[4,32,128]{2,1,0:T(8,128)}, u32[]{:S(2)}) copy-start(f32[4,32,128]{2,1,0:T(8,128)} %get-tuple-element.2579) | copy-start | bytes 196612
  285.5 362.8 %all-gather.26.cloned.1.call-start = ((), (), s32[]{:S(2)}) async-start(), calls=%async_computation.2 | async-start | bytes 2162688 | tf_op jit(solution)/shard_map/all_gather | solution.py:102
  725.8 0.6 copy-start.3
Sparse Core Ops, SparseCore 0:
  10.5 88.6 all-gather.21
  285.7 79.2 all-gather.23
  569.1 79.2 all-gather.25
where the time goes:
time: 741 us; the launch traced here: 733 us
  other arithmetic  264 us (36%)
  waiting for transfers between devices  247 us (33%)
  blocking collectives  124 us (17%)
  local copies, waits for them, and re-layouts  73.4 us (10%)
  between operations  14.4 us (2%)
  loops' own time  10.6 us (1%)
    all_gather x2, waiting for transfers between devices, chain(): all_corrections = lax.all_gather(correction[None], 'tm', axis=0, tiled=True)  159 us
    all_gather x8, blocking collectives, couple(): gathered = lax.all_gather(exported, 'frac', axis=0, tiled=True)  124 us
    all_gather x1, waiting for transfers between devices, body(): all_sources = lax.all_gather(sources, 'tm', axis=0, tiled=True)  88 us
    add x94, other arithmetic, implicit(): right_side = storage_rate * pressure + slice_source  82.8 us
    select_n x93, other arithmetic, turn(): kept_state = jnp.where(slice_index == turn_index + 1, current, kept_state)  55 us
    gather x8, local copies, waits for them, and re-layouts, couple(): remote_values = gathered[trace_source]  49.2 us
    scatter-add x8, other arithmetic, couple(): return jnp.zeros_like(flat_field).at[inter_local].add(weights * remote_va...  47.6 us
    div x254, other arithmetic, sweep(): return (right_side + beside) / diagonal_total  25 us
  transfers between devices with their start and end apart: 3, of which 3 were waited for; matrix products, arithmetic and copies ran while one was open for 0% of the time, Pallas kernels for 0%

commit v1 on v0

--- a/solution.py
+++ b/solution.py
@@ -99,7 +99,11 @@
         if carry_zero:
             all_corrections = jnp.zeros_like(all_sources)
         else:
-            all_corrections = lax.all_gather(correction[None], "tm", axis=0, tiled=True)
+            length = lax.axis_size("tm")
+            repeats = [length if d == 0 else 1 for d in range(correction[None].ndim)]
+            all_corrections = lax.all_to_all(
+                jnp.tile(correction[None], repeats), "tm", split_axis=0, concat_axis=0, tiled=True
+            )
 
         def turn(turn_index, carried):
             current, kept_state = carried

time: 741 us -> 640 us (0.86)
  the two profiles are of different devices: /device:TPU:8 before, /device:TPU:5 now
where the time goes in v1:
time: 640 us; the launch traced here: 635 us
  other arithmetic  210 us (33%)
  waiting for transfers between devices  182 us (28%)
  blocking collectives  128 us (20%)
  local copies, waits for them, and re-layouts  76.7 us (12%)
  between operations  14.7 us (2%)
  starting transfers between devices  12.3 us (2%)
  loops' own time  10.8 us (2%)
    all_gather x8, blocking collectives, couple(): gathered = lax.all_gather(exported, 'frac', axis=0, tiled=True)  128 us
    all_to_all x2, waiting for transfers between devices, chain(): lax.all_to_all(jnp.tile(correction[None], repeats), 'tm', split_axis=0, c...  99.9 us
    add x94, other arithmetic, implicit(): right_side = storage_rate * pressure + slice_source  82.8 us
    all_gather x1, waiting for transfers between devices, body(): all_sources = lax.all_gather(sources, 'tm', axis=0, tiled=True)  82.3 us
    gather x8, local copies, waits for them, and re-layouts, couple(): remote_values = gathered[trace_source]  49.2 us
    scatter-add x8, other arithmetic, couple(): return jnp.zeros_like(flat_field).at[inter_local].add(weights * remote_va...  47.6 us
    div x254, other arithmetic, sweep(): return (right_side + beside) / diagonal_total  25 us
    slice x254, other arithmetic, next_cols(): array[:, :, 1:]  20.6 us
  transfers between devices with their start and end apart: 3, of which 3 were waited for; matrix products, arithmetic and copies ran while one was open for 0% of the time, Pallas kernels for 0%

profile of v1, /device:TPU:5, one launch (start us, length us, event | category | flops | bytes accessed | tf_op | source)
XLA Modules:
  0.0 634.8 jit_solution(13973755785336166617)
XLA Ops:
  11.1 82.3 %all-gather.18.cloned.1.call-done = f32[32,4,32,128]{3,2,1,0:T(8,128)} async-done(((f32[1,4,32,128]{3,2,1,0:T(8,128)}), f32[32,4,32,128]{3,2,1,0:T(8,128)}) %all-gather.18.cloned.1.call-update) | async-done | bytes 2097168 | tf_op jit(solution)/shard_map/all_gather | solution.py:96
  93.4 52.9 %while.235 = (s32[]{:T(128)}, f32[4,32,128]{2,1,0:T(8,128)S(1)}, f32[4,32,128]{2,1,0:T(8,128)S(1)}, f32[4,32,128]{2,1,0:T(8,128)}, f32[4,32,128]{2,1,0:T(8,128)}...) while((s32[]{:T(128)}, f32[4,32,128]{2,1,0:T(8,128)S(1)}, ...), condition=%wide.region_3.4_spmd, body=%wide.region_0.3_spmd.sunk | while | flops 392741 | bytes 2790472 | solution.py:116
  147.3 1.7 gather_fusion
  149.0 21.9 %all-gather.8 = f32[16,1,256]{2,1,0:T(1,128)S(1)} all-gather(f32[1,1,256]{2,1,0:T(1,128)S(1)} %bitcast.170), channel_id=2, replica_groups=mesh['tm'=32,'frac'=16] {'frac'}, dimensions={0}, use_global_device_ids=true | all-gather | bytes 17408 | tf_op jit(solution)/shard_map/all_gather | solution.py:84
  170.9 6.2 gather_fusion.1
  177.1 5.9 scatter_custom_fusion.1
  183.1 5.9 scatter_custom_fusion
  189.2 1.7 while.236
  190.9 1.7 gather_fusion.2
  192.7 15.2 %all-gather.9 = f32[16,1,256]{2,1,0:T(1,128)S(1)} all-gather(f32[1,1,256]{2,1,0:T(1,128)S(1)} %bitcast.171), channel_id=3, replica_groups=mesh['tm'=32,'frac'=16] {'frac'}, dimensions={0}, use_global_device_ids=true | all-gather | bytes 17408 | tf_op jit(solution)/shard_map/all_gather | solution.py:84
  207.9 6.1 gather_fusion.3
  214.1 5.9 scatter_custom_fusion.2
  220.3 1.7 while.237
  222.1 1.7 gather_fusion.4
  223.8 15.1 %all-gather.10 = f32[16,1,256]{2,1,0:T(1,128)S(1)} all-gather(f32[1,1,256]{2,1,0:T(1,128)S(1)} %bitcast.172), channel_id=4, replica_groups=mesh['tm'=32,'frac'=16] {'frac'}, dimensions={0}, use_global_device_ids=true | all-gather | bytes 17408 | tf_op jit(solution)/shard_map/all_gather | solution.py:84
  238.9 6.1 gather_fusion.5
  245.0 5.9 scatter_custom_fusion.3
  251.3 1.7 while.238
  253.0 1.7 gather_fusion.6
  254.8 15.2 %all-gather.11 = f32[16,1,256]{2,1,0:T(1,128)S(1)} all-gather(f32[1,1,256]{2,1,0:T(1,128)S(1)} %bitcast.173), channel_id=5, replica_groups=mesh['tm'=32,'frac'=16] {'frac'}, dimensions={0}, use_global_device_ids=true | all-gather | bytes 17408 | tf_op jit(solution)/shard_map/all_gather | solution.py:84
  270.0 6.1 gather_fusion.7
  276.2 5.9 scatter_custom_fusion.4
  282.8 1.7 while.239
  286.2 6.6 %all-to-all-start = ((f32[32,4,32,128]{3,2,1,0:T(8,128)}), f32[32,4,32,128]{3,2,1,0:T(8,128)S(1)}, u32[]{:S(2)}, u32[]{:S(2)}) async-start(f32[32,4,32,128]{3,2,1,0:T(8,128)} %tile.4), calls=%async_computation | async-start | bytes 4194304 | tf_op jit(solution)/shard_map/all_to_all | solution.py:104
  292.8 49.9 %all-to-all-done = f32[32,4,32,128]{3,2,1,0:T(8,128)S(1)} async-done(((f32[32,4,32,128]{3,2,1,0:T(8,128)}), f32[32,4,32,128]{3,2,1,0:T(8,128)S(1)}, u32[]{:S(2)}, u32[]{:S(2)}) %all-to-all-start) | async-done | bytes 2097184 | tf_op jit(solution)/shard_map/all_to_all | solution.py:104
  342.7 51.1 %while.242 = (s32[]{:T(128)}, f32[4,32,128]{2,1,0:T(8,128)S(1)}, f32[4,32,128]{2,1,0:T(8,128)S(1)}, f32[4,32,128]{2,1,0:T(8,128)S(1)}, f32[4,32,128]{2,1,0:T(8,1...) while((s32[]{:T(128)}, f32[4,32,128]{2,1,0:T(8,128)S(1)}, ...), condition=%wide.region_22.23_spmd, body=%wide.region_19.22_spmd.sunk | while | flops 409125 | bytes 2921564 | solution.py:116
  393.9 1.7 gather_fusion.8
  395.6 15.4 %all-gather.12 = f32[16,1,256]{2,1,0:T(1,128)S(1)} all-gather(f32[1,1,256]{2,1,0:T(1,128)S(1)} %bitcast.174), channel_id=6, replica_groups=mesh['tm'=32,'frac'=16] {'frac'}, dimensions={0}, use_global_device_ids=true | all-gather | bytes 17408 | tf_op jit(solution)/shard_map/all_gather | solution.py:84
  411.1 6.1 gather_fusion.9
  417.2 5.9 scatter_custom_fusion.5
  423.5 1.7 while.243
  425.2 1.7 gather_fusion.10
  426.9 15.2 %all-gather.13 = f32[16,1,256]{2,1,0:T(1,128)S(1)} all-gather(f32[1,1,256]{2,1,0:T(1,128)S(1)} %bitcast.175), channel_id=7, replica_groups=mesh['tm'=32,'frac'=16] {'frac'}, dimensions={0}, use_global_device_ids=true | all-gather | bytes 17408 | tf_op jit(solution)/shard_map/all_gather | solution.py:84
  442.2 6.1 gather_fusion.11
  448.3 5.9 scatter_custom_fusion.6
  456.3 1.7 gather_fusion.12
  458.1 15.1 %all-gather.14 = f32[16,1,256]{2,1,0:T(1,128)S(1)} all-gather(f32[1,1,256]{2,1,0:T(1,128)S(1)} %bitcast.176), channel_id=8, replica_groups=mesh['tm'=32,'frac'=16] {'frac'}, dimensions={0}, use_global_device_ids=true | all-gather | bytes 17408 | tf_op jit(solution)/shard_map/all_gather | solution.py:84
  473.2 6.1 gather_fusion.13
  479.3 5.9 scatter_custom_fusion.7
  485.6 1.7 while.245
  487.3 1.7 gather_fusion.14
  489.0 15.2 %all-gather.15 = f32[16,1,256]{2,1,0:T(1,128)S(1)} all-gather(f32[1,1,256]{2,1,0:T(1,128)S(1)} %bitcast.169), channel_id=9, replica_groups=mesh['tm'=32,'frac'=16] {'frac'}, dimensions={0}, use_global_device_ids=true | all-gather | bytes 17408 | tf_op jit(solution)/shard_map/all_gather | solution.py:84
  504.3 6.1 gather_fusion.15
  510.4 5.9 scatter_custom_fusion.8
  517.1 1.7 while.246
  520.5 5.7 all-to-all-start.1
  526.2 49.9 %all-to-all-done.1 = f32[32,4,32,128]{3,2,1,0:T(8,128)S(1)} async-done(((f32[32,4,32,128]{3,2,1,0:T(8,128)}), f32[32,4,32,128]{3,2,1,0:T(8,128)S(1)}, u32[]{:S(2)}, u32[]{:S(2)}) %all-to-all-start.1) | async-done | bytes 2097184 | tf_op jit(solution)/shard_map/all_to_all | solution.py:104
  576.2 51.1 %while.249 = (s32[]{:T(128)}, f32[4,32,128]{2,1,0:T(8,128)S(1)}, f32[4,32,128]{2,1,0:T(8,128)S(1)}, f32[4,32,128]{2,1,0:T(8,128)S(1)}, f32[4,32,128]{2,1,0:T(8,1...) while((s32[]{:T(128)}, f32[4,32,128]{2,1,0:T(8,128)S(1)}, ...), condition=%wide.region_40.41_spmd, body=%wide.region_37.40_spmd.sunk | while | flops 409125 | bytes 2921564 | solution.py:116
  (1683 shorter events, 212.3 us)
Async XLA Ops:
  6.5 86.8 %all-gather.18.cloned.1.call-start = ((), (), s32[]{:S(2)}) async-start(), calls=%async_computation.2 | async-start | bytes 2162688 | tf_op jit(solution)/shard_map/all_gather | solution.py:96
  170.9 6.2 copy-start.5
  170.9 18.2 %copy-start = (f32[4,32,128]{2,1,0:T(8,128)S(1)}, f32[4,32,128]{2,1,0:T(8,128)}, u32[]{:S(2)}) copy-start(f32[4,32,128]{2,1,0:T(8,128)} %get-tuple-element.2571) | copy-start | bytes 196612
  170.9 18.2 %copy-start.2 = (f32[1,4,32,128]{3,2,1,0:T(8,128)S(1)}, f32[1,4,32,128]{3,2,1,0:T(8,128)}, u32[]{:S(2)}) copy-start(f32[1,4,32,128]{3,2,1,0:T(8,128)} %param.46) | copy-start | bytes 196612
  170.9 18.2 %copy-start.4 = (f32[4,32,128]{2,1,0:T(8,128)S(1)}, f32[4,32,128]{2,1,0:T(8,128)}, u32[]{:S(2)}) copy-start(f32[4,32,128]{2,1,0:T(8,128)} %param.45) | copy-start | bytes 196612
  207.9 12.1 %copy-start.1 = (f32[4,32,128]{2,1,0:T(8,128)S(1)}, f32[4,32,128]{2,1,0:T(8,128)}, u32[]{:S(2)}) copy-start(f32[4,32,128]{2,1,0:T(8,128)} %get-tuple-element.2577) | copy-start | bytes 196612
  286.2 56.5 %all-to-all-start = ((f32[32,4,32,128]{3,2,1,0:T(8,128)}), f32[32,4,32,128]{3,2,1,0:T(8,128)S(1)}, u32[]{:S(2)}, u32[]{:S(2)}) async-start(f32[32,4,32,128]{3,2,1,0:T(8,128)} %tile.4), calls=%async_computation | async-start | bytes 4194304 | tf_op jit(solution)/shard_map/all_to_all | solution.py:104
  520.5 55.7 %all-to-all-start.1 = ((f32[32,4,32,128]{3,2,1,0:T(8,128)}), f32[32,4,32,128]{3,2,1,0:T(8,128)S(1)}, u32[]{:S(2)}, u32[]{:S(2)}) async-start(f32[32,4,32,128]{3,2,1,0:T(8,128)} %tile.5), calls=%async_computation.1 | async-start | bytes 4194304 | tf_op jit(solution)/shard_map/all_to_all | solution.py:104
  627.3 0.6 copy-start.3
Sparse Core Ops, SparseCore 0:
  10.5 82.8 all-gather.17
